TPU v7x, 32 devices: a whole 2x2x4 slice. The times are simulated.
32 devices in a mesh: chan: 16 (over z, x, core), tm: 2 (over y).
Axes of the slice: x: 2, y: 2, z: 4, core: 2. Of those that a mesh axis runs over, the one named last changes fastest.
Arguments:
- samples: bfloat16 [96, 2, 2048], P('chan', 'tm'), may hold values from -6 to 6
- dead_flags: int32 [96], P('chan'), may hold values 0 or 1
- pair_mask: int32 [96, 96], P('chan', 'tm'), may hold values 0 or 1
Outputs:
- xcorr: float32 [96, 96, 301], P('chan', 'tm')
All inputs are finite; a program needn't handle non-finite values. No bound on the sum of `dead_flags` or of `pair_mask` on one device may be relied on, other than what follows from the above.
Results may differ from a plain program's by a relative error of at most 0.0095.
Values may be sent and summed in bfloat16 or wider, within the bound.
A program may use at most 64 MiB of HBM per device.

v0:
```python
import math
import jax
import jax.numpy as jnp
from jax import lax
from jax.sharding import PartitionSpec as P

F = 768
LAGS = 301


def taper_window(length):
    sample_index = jnp.arange(length, dtype=jnp.float32)
    return 0.5 - 0.5 * jnp.cos(2.0 * math.pi * (sample_index + 0.5) / length)


def forward_table(length, bins):
    sample_index = jnp.arange(length, dtype=jnp.int32)
    frequency = jnp.arange(1, bins + 1, dtype=jnp.int32)
    phase_index = sample_index[:, None] * frequency[None, :] % length
    angles = 2.0 * math.pi / length * phase_index.astype(jnp.float32)
    return jnp.concatenate([jnp.cos(angles), -jnp.sin(angles)], axis=1).astype(jnp.bfloat16)


def lag_table(length, bins, lags, factor):
    frequency = jnp.arange(1, bins + 1, dtype=jnp.int32)
    shifts = jnp.arange(lags, dtype=jnp.int32) - (lags - 1) // 2
    phase_index = jnp.mod(frequency[:, None] * shifts[None, :], length)
    angles = 2.0 * math.pi / length * phase_index.astype(jnp.float32)
    table_values = jnp.concatenate([jnp.cos(angles), -jnp.sin(angles)], axis=0) * factor
    return table_values.astype(jnp.bfloat16)


def whiten(samples, dead_flags, table_values):
    channel_count, windows, length = samples.shape
    bins = table_values.shape[1] // 2
    traces = samples.astype(jnp.float32)
    traces = traces - jnp.mean(traces, axis=-1, keepdims=True)
    tapered = (traces * taper_window(length)).astype(jnp.bfloat16)
    spectra = jnp.dot(
        tapered.reshape(channel_count * windows, length),
        table_values,
        preferred_element_type=jnp.float32,
    )
    real_part = spectra[:, :bins]
    imag_part = spectra[:, bins:]
    energy = real_part * real_part + imag_part * imag_part
    mean_energy = jnp.mean(energy, axis=-1, keepdims=True)
    inverse_scale = lax.rsqrt(energy + 0.25 * mean_energy + 1e-06)
    alive_rows = jnp.repeat((1 - dead_flags).astype(jnp.float32), windows)[:, None]
    whitened = (
        jnp.concatenate([real_part * inverse_scale, imag_part * inverse_scale], axis=1) * alive_rows
    )
    return whitened.astype(jnp.bfloat16).reshape(channel_count, windows, 2 * bins)


def correlate(receivers, sources, lag_weights):
    bins = receivers.shape[-1] // 2
    rec_values = receivers.astype(jnp.float32)
    src_values = sources.astype(jnp.float32)
    rec_re = rec_values[:, None, :, :bins]
    rec_im = rec_values[:, None, :, bins:]
    src_re = src_values[None, :, :, :bins]
    src_im = src_values[None, :, :, bins:]
    cross_re = rec_re * src_re + rec_im * src_im
    cross_im = rec_im * src_re - rec_re * src_im
    cross = jnp.concatenate([cross_re, cross_im], axis=-1).astype(jnp.bfloat16)
    result = jnp.einsum("rgwk,kl->wrgl", cross, lag_weights, preferred_element_type=jnp.float32)
    return result.astype(jnp.bfloat16)


def pick_group(source_count, rows_each):
    chosen = 1
    for candidate in range(1, source_count + 1):
        if source_count % candidate == 0 and candidate * rows_each <= 1024:
            chosen = candidate
    return chosen


def per_device(samples, dead_flags, pair_mask):
    block_size, local_windows, length = samples.shape
    table_values = forward_table(length, F)
    whitened = whiten(samples, dead_flags, table_values)
    subwin = local_windows * lax.axis_size("tm")
    lag_weights = lag_table(length, F, LAGS, 1.0 / math.sqrt(subwin * F))
    incoming = lax.all_gather(whitened, "chan", axis=0, tiled=True)
    source_count = incoming.shape[0]
    group_size = pick_group(source_count, block_size * local_windows)
    grouped = incoming.reshape(source_count // group_size, group_size, local_windows, 2 * F)

    def one_group(group_sources):
        return correlate(whitened, group_sources, lag_weights)[0]

    results = lax.map(one_group, grouped)
    placed = jnp.transpose(results, (1, 0, 2, 3)).reshape(block_size, source_count, LAGS)
    shares = lax.psum_scatter(
        placed.astype(jnp.float32).astype(jnp.bfloat16), "tm", scatter_dimension=1, tiled=True
    ).astype(jnp.float32)
    return shares * pair_mask.astype(jnp.float32)[..., None]


def solution(mesh):
    in_specs = (P("chan", "tm", None), P("chan"), P("chan", "tm"))
    out_specs = P("chan", "tm", None)
    return jax.shard_map(
        per_device, mesh=mesh, in_specs=in_specs, out_specs=out_specs, check_vma=False
    )
```

profile of v0, /device:TPU:0, one launch (start us, length us, event | category | flops | bytes accessed | tf_op | source)
XLA Modules:
  0.0 85.0 jit_solution(8352473777845611654)
XLA Ops:
  6.5 0.0 reduce-scatter.2.cloned.1.call-start
  6.5 0.1 multiply_subtract_fusion
  6.6 0.0 copy-start
  6.6 25.4 %cosine_convert_fusion = (bf16[2048,768]{1,0:T(8,128)(2,1)S(1)}, bf16[2048,768]{1,0:T(8,128)(2,1)S(1)}) fusion(s32[768]{0:T(1024)S(1)} %iota_add_fusion), kind=kLoop, calls=%fused_computation.11 | loop fusion | flops 26738688 | bytes 6294528 | tf_op jit(solution)/shard_map/convert.2
  32.1 0.0 copy-done
  32.1 0.1 convert_reduce_fusion
  32.2 0.0 copy-start.2
  32.2 1.0 %fusion.3 = f32[6,1536]{1,0:T(8,128)S(1)} fusion(bf16[2048,768]{1,0:T(8,128)(2,1)S(1)} %get-tuple-element.33, bf16[2048,768]{1,0:T(8,128)(2,1)S(1)} %get-tuple-element.32, bf16[6,1,2048]{2,0,1:T(8,128)(2,1)S(1)} %copy-done, f32[2048]{0:T(1024)S(1)} %multiply_subtract_fusion, f32[6]{0:T(128)S(1)} %broadcast_multiply_fusion.1), kind=kOutput, calls=%fused_computation.6 | convolution fusion | flops 50380800 | bytes 6361112 | tf_op jit(solution)/shard_map/dot_general | solution.py:39
  33.2 0.1 fusion.39
  33.3 0.1 multiply_bitcast_fusion.1
  33.4 0.0 copy-done.2
  33.4 0.1 fusion.40
  33.5 24.9 %all_gather.3 = bf16[96,1,1536]{2,1,0:T(2,128)(2,1)S(1)} all-gather(bf16[6,1,1536]{2,1,0:T(2,128)(2,1)S(1)} %copy.4), channel_id=1, replica_groups=mesh['chan'=16,'tm'=2] {'chan'}, dimensions={0}, use_global_device_ids=true | all-gather | bytes 313344 | tf_op jit(solution)/shard_map/all_gather | solution.py:85
  58.4 0.6 fusion.42
  59.0 3.7 %fusion.27 = (f32[768,301]{0,1:T(8,128)S(1)}, f32[768,301]{0,1:T(8,128)S(1)}) fusion(s32[301]{0:T(512)S(1)} %iota_add_fusion.1, s32[768]{0:T(1024)S(1)} %iota_add_fusion), kind=kLoop, calls=%fused_computation.36 | loop fusion | flops 3467520 | bytes 1853620 | tf_op jit(solution)/shard_map/cos | solution.py:29
  62.8 0.5 add_convert_fusion
  63.3 0.0 copy-start.1
  63.3 1.9 %fusion.18 = bf16[6,96,301]{2,1,0:T(8,128)(2,1)} fusion(bf16[6,96,768]{2,1,0:T(8,128)(2,1)S(1)} %get-tuple-element.22, bf16[6,96,768]{2,1,0:T(8,128)(2,1)S(1)} %get-tuple-element.20, f32[768,301]{0,1:T(8,128)S(1)} %get-tuple-element.31, f32[768,301]{0,1:T(8,128)S(1)} %get-tuple-element.30), kind=kOutput, calls=%fused_computation.29 | convolution fusion | flops 537710400 | bytes 3965568 | tf_op jit(solution)/shard_map/while/body/eval_jaxpr/rgwk,kl->wrgl/dot_general | solution.py:67
  65.2 0.0 reduce-scatter.2.cloned.1.call-update
  65.2 0.0 copy-done.1
  65.2 11.2 %reduce-scatter.2.cloned.1.call-done = bf16[6,48,301]{2,1,0:T(8,128)(2,1)} async-done(((bf16[6,96,301]{2,1,0:T(8,128)(2,1)}), bf16[6,48,301]{2,1,0:T(8,128)(2,1)}) %reduce-scatter.2.cloned.1.call-update) | async-done | bytes 173392 | tf_op jit(solution)/shard_map/reduce_scatter | solution.py:95
  76.4 1.8 %convert_multiply_fusion = f32[6,48,301]{2,1,0:T(8,128)} fusion(bf16[6,48,301]{2,1,0:T(8,128)(2,1)} %reduce-scatter.2.cloned.1.call-done, f32[6,48]{1,0:T(8,128)S(1)} %convert_element_type.91), kind=kLoop, calls=%fused_computation.37 | loop fusion | flops 173376 | bytes 521280 | tf_op jit(solution)/shard_map/mul | solution.py:98
  (9 shorter events, 0.1 us)
Async XLA Ops:
  6.5 69.9 %reduce-scatter.2.cloned.1.call-start = ((), (), s32[]{:S(2)}) async-start(), calls=%async_computation.1 | async-start | bytes 663552 | tf_op jit(solution)/shard_map/reduce_scatter | solution.py:95
  6.6 25.5 %copy-start = (bf16[6,1,2048]{2,0,1:T(8,128)(2,1)S(1)}, bf16[6,1,2048]{2,0,1:T(8,128)(2,1)}, u32[]{:S(2)}) copy-start(bf16[6,1,2048]{2,0,1:T(8,128)(2,1)} %param.3) | copy-start | bytes 73732
  32.2 1.2 %copy-start.2 = (s32[6]{0:T(128)S(1)}, s32[6]{0:T(128)}, u32[]{:S(2)}) copy-start(s32[6]{0:T(128)} %param.4) | copy-start | bytes 76
  63.3 1.9 %copy-start.1 = (s32[6,48]{1,0:T(8,128)S(1)}, s32[6,48]{1,0:T(8,128)}, u32[]{:S(2)}) copy-start(s32[6,48]{1,0:T(8,128)} %param.5) | copy-start | bytes 3460
Sparse Core Ops, SparseCore 0:
  65.3 11.0 reduce-scatter.1
where the time goes:
time: 85.2 us; the launch traced here: 85 us
  other arithmetic  32 us (38%)
  blocking collectives  24.9 us (29%)
  between operations  13.5 us (16%)
  waiting for transfers between devices  11.2 us (13%)
  matrix products  2.82 us (3%)
    another operation x2, other arithmetic  25.9 us
    all_gather x1, blocking collectives, per_device(): incoming = lax.all_gather(whitened, 'chan', axis=0, tiled=True)  24.9 us
    reduce_scatter x1, waiting for transfers between devices, per_device(): lax.psum_scatter(placed.astype(jnp.float32).astype(jnp.bfloat16), 'tm', s...  11.2 us
    cos x1, other arithmetic, lag_table(): jnp.cos(angles)  3.74 us
    dot_general x1, matrix products, correlate(): jnp.einsum('rgwk,kl->wrgl', cross, lag_weights, preferred_element_type=jn...  1.86 us
    mul x1, other arithmetic, per_device(): return shares * pair_mask.astype(jnp.float32)[..., None]  1.8 us
  transfers between devices with their start and end apart: 1, of which 1 were waited for; matrix products, arithmetic and copies ran while one was open for 0% of the time, Pallas kernels for 0%

commit v1 on v0

--- a/solution.py
+++ b/solution.py
@@ -6,6 +6,18 @@
 
 F = 768
 LAGS = 301
+
+
+def collect(shard, axis, dim):
+    ways, here = (lax.axis_size(axis), lax.axis_index(axis))
+    grown, reach = (shard, 1)
+    while reach < ways:
+        theirs = lax.ppermute(grown, axis, [(d, d ^ reach) for d in range(ways)])
+        mine_first = jnp.concatenate([grown, theirs], axis=dim)
+        theirs_first = jnp.concatenate([theirs, grown], axis=dim)
+        grown = jnp.where(here & reach == 0, mine_first, theirs_first)
+        reach = 2 * reach
+    return grown
 
 
 def taper_window(length):
@@ -82,7 +94,7 @@
     whitened = whiten(samples, dead_flags, table_values)
     subwin = local_windows * lax.axis_size("tm")
     lag_weights = lag_table(length, F, LAGS, 1.0 / math.sqrt(subwin * F))
-    incoming = lax.all_gather(whitened, "chan", axis=0, tiled=True)
+    incoming = collect(whitened, "chan", 0)
     source_count = incoming.shape[0]
     group_size = pick_group(source_count, block_size * local_windows)
     grouped = incoming.reshape(source_count // group_size, group_size, local_windows, 2 * F)

time: 85.2 us -> 82.3 us (0.966)
  blocking collectives: 24.9 us -> 0 us
  waiting for transfers between devices: 11.2 us -> 25.5 us
  starting transfers between devices: 0.01 us -> 7.85 us
    all_gather x1 -> x0, blocking collectives: 24.9 us -> none  [per_device(): incoming = lax.all_gather(whitened, 'chan', axis=0, tiled=True)]
    ppermute x0 -> x4, waiting for transfers between devices: none -> 10.6 us  [collect(): theirs = lax.ppermute(grown, axis, [(d, d ^ reach) for d in range(ways)])]
    ppermute x0 -> x4, starting transfers between devices: none -> 7.85 us  [collect(): theirs = lax.ppermute(grown, axis, [(d, d ^ reach) for d in range(ways)])]
    reduce_scatter x1, waiting for transfers between devices: 11.2 us -> 15 us  [per_device(): lax.psum_scatter(placed.astype(jnp.float32).astype(jnp.bfloat16), 'tm', s...]
  transfers between devices with their start and end apart: 1 -> 5, of which waited for: 1 -> 4; matrix products, arithmetic and copies ran while one was open for 0% -> 5% of each run, Pallas kernels for 0% -> 0%
where the time goes in v1:
time: 82.3 us; the launch traced here: 82.1 us
  other arithmetic  32.3 us (39%)
  waiting for transfers between devices  25.5 us (31%)
  between operations  13.6 us (17%)
  starting transfers between devices  7.85 us (10%)
  matrix products  2.83 us (3%)
    another operation x2, other arithmetic  25.9 us
    reduce_scatter x1, waiting for transfers between devices, per_device(): lax.psum_scatter(placed.astype(jnp.float32).astype(jnp.bfloat16), 'tm', s...  15 us
    ppermute x4, waiting for transfers between devices, collect(): theirs = lax.ppermute(grown, axis, [(d, d ^ reach) for d in range(ways)])  10.6 us
    ppermute x4, starting transfers between devices, collect(): theirs = lax.ppermute(grown, axis, [(d, d ^ reach) for d in range(ways)])  7.85 us
    cos x1, other arithmetic, lag_table(): jnp.cos(angles)  3.73 us
    dot_general x1, matrix products, correlate(): jnp.einsum('rgwk,kl->wrgl', cross, lag_weights, preferred_element_type=jn...  1.87 us
    mul x1, other arithmetic, per_device(): return shares * pair_mask.astype(jnp.float32)[..., None]  1.8 us
  transfers between devices with their start and end apart: 5, of which 4 were waited for; matrix products, arithmetic and copies ran while one was open for 5% of the time, Pallas kernels for 0%

profile of v1, /device:TPU:0, one launch (start us, length us, event | category | flops | bytes accessed | tf_op | source)
XLA Modules:
  0.0 82.1 jit_solution(13820353604542867922)
XLA Ops:
  6.5 0.0 reduce-scatter.2.cloned.1.call-start
  6.5 0.1 multiply_subtract_fusion
  6.6 0.0 copy-start
  6.6 25.4 %cosine_convert_fusion = (bf16[2048,768]{1,0:T(8,128)(2,1)S(1)}, bf16[2048,768]{1,0:T(8,128)(2,1)S(1)}) fusion(s32[768]{0:T(1024)S(1)} %iota_add_fusion), kind=kLoop, calls=%fused_computation.11 | loop fusion | flops 26738688 | bytes 6294528 | tf_op jit(solution)/shard_map/convert.2
  32.1 0.0 copy-done
  32.1 0.1 convert_reduce_fusion
  32.2 0.0 copy-start.2
  32.2 1.0 %fusion.3 = f32[6,1536]{1,0:T(8,128)S(1)} fusion(bf16[2048,768]{1,0:T(8,128)(2,1)S(1)} %get-tuple-element.33, bf16[2048,768]{1,0:T(8,128)(2,1)S(1)} %get-tuple-element.32, bf16[6,1,2048]{2,0,1:T(8,128)(2,1)S(1)} %copy-done, f32[2048]{0:T(1024)S(1)} %multiply_subtract_fusion, f32[6]{0:T(128)S(1)} %broadcast_multiply_fusion.1), kind=kOutput, calls=%fused_computation.6 | convolution fusion | flops 50380800 | bytes 6361112 | tf_op jit(solution)/shard_map/dot_general | solution.py:51
  33.2 0.1 fusion.42
  33.3 0.1 slice_multiply_fusion.1
  33.4 0.0 copy-done.2
  33.4 0.1 fusion.43
  33.5 0.5 collective-permute-start
  34.0 0.1 fusion.33
  34.1 3.7 %fusion.27 = (f32[768,301]{0,1:T(8,128)S(1)}, f32[768,301]{0,1:T(8,128)S(1)}) fusion(s32[301]{0:T(512)S(1)} %iota_add_fusion.1, s32[768]{0:T(1024)S(1)} %iota_add_fusion), kind=kLoop, calls=%fused_computation.36 | loop fusion | flops 3467520 | bytes 1853620 | tf_op jit(solution)/shard_map/cos | solution.py:41
  37.9 0.0 collective-permute-done
  37.9 2.6 %collective-permute-start.1 = (bf16[12,1,1536]{2,0,1:T(8,128)(2,1)S(1)}, bf16[12,1,1536]{2,0,1:T(8,128)(2,1)S(1)}, u32[]{:S(2)}, u32[]{:S(2)}) collective-permute-start(bf16[12,1,1536]{2,0,1:T(8,128)(2,1)S(1)} %maximum_select_fusion.6), channel_id=1, source_target_pairs={{0,4},{2,6},{4,0},{6,2},{8,12},{10,14},{12,8},{14,10},{16,20},{18,... | collective-permute-start | bytes 110600 | tf_op jit(solution)/shard_map/ppermute | solution.py:15
  40.5 2.4 %collective-permute-done.1 = bf16[12,1,1536]{2,0,1:T(8,128)(2,1)S(1)} collective-permute-done((bf16[12,1,1536]{2,0,1:T(8,128)(2,1)S(1)}, bf16[12,1,1536]{2,0,1:T(8,128)(2,1)S(1)}, u32[]{:S(2)}, u32[]{:S(2)}) %collective-permute-start.1) | collective-permute-done | bytes 36896 | tf_op jit(solution)/shard_map/ppermute | solution.py:15
  42.9 1.9 %collective-permute-start.2 = (bf16[24,1,1536]{2,0,1:T(8,128)(2,1)S(1)}, bf16[24,1,1536]{2,0,1:T(8,128)(2,1)S(1)}, u32[]{:S(2)}, u32[]{:S(2)}) collective-permute-start(bf16[24,1,1536]{2,0,1:T(8,128)(2,1)S(1)} %maximum_select_fusion.4), channel_id=1, source_target_pairs={{0,8},{2,10},{4,12},{6,14},{8,0},{10,2},{12,4},{14,6},{16,24},{18,... | collective-permute-start | bytes 221192 | tf_op jit(solution)/shard_map/ppermute | solution.py:15
  44.8 2.5 %collective-permute-done.2 = bf16[24,1,1536]{2,0,1:T(8,128)(2,1)S(1)} collective-permute-done((bf16[24,1,1536]{2,0,1:T(8,128)(2,1)S(1)}, bf16[24,1,1536]{2,0,1:T(8,128)(2,1)S(1)}, u32[]{:S(2)}, u32[]{:S(2)}) %collective-permute-start.2) | collective-permute-done | bytes 73760 | tf_op jit(solution)/shard_map/ppermute | solution.py:15
  47.4 2.9 %collective-permute-start.3 = (bf16[48,1,1536]{2,0,1:T(8,128)(2,1)S(1)}, bf16[48,1,1536]{2,0,1:T(8,128)(2,1)S(1)}, u32[]{:S(2)}, u32[]{:S(2)}) collective-permute-start(bf16[48,1,1536]{2,0,1:T(8,128)(2,1)S(1)} %maximum_select_fusion.2), channel_id=1, source_target_pairs={{0,16},{2,18},{4,20},{6,22},{8,24},{10,26},{12,28},{14,30},{16,0},... | collective-permute-start | bytes 442376 | tf_op jit(solution)/shard_map/ppermute | solution.py:15
  50.3 5.7 %collective-permute-done.3 = bf16[48,1,1536]{2,0,1:T(8,128)(2,1)S(1)} collective-permute-done((bf16[48,1,1536]{2,0,1:T(8,128)(2,1)S(1)}, bf16[48,1,1536]{2,0,1:T(8,128)(2,1)S(1)}, u32[]{:S(2)}, u32[]{:S(2)}) %collective-permute-start.3) | collective-permute-done | bytes 147488 | tf_op jit(solution)/shard_map/ppermute | solution.py:15
  56.1 0.5 add_convert_fusion
  56.6 0.0 copy-start.1
  56.6 1.9 %fusion.18 = bf16[6,96,301]{2,1,0:T(8,128)(2,1)} fusion(bf16[6,96,768]{2,1,0:T(8,128)(2,1)S(1)} %get-tuple-element.22, bf16[6,96,768]{2,1,0:T(8,128)(2,1)S(1)} %get-tuple-element.20, f32[768,301]{0,1:T(8,128)S(1)} %get-tuple-element.31, f32[768,301]{0,1:T(8,128)S(1)} %get-tuple-element.30), kind=kOutput, calls=%fused_computation.29 | convolution fusion | flops 537710400 | bytes 3965568 | tf_op jit(solution)/shard_map/while/body/eval_jaxpr/rgwk,kl->wrgl/dot_general | solution.py:79
  58.5 0.0 reduce-scatter.2.cloned.1.call-update
  58.5 0.0 copy-done.1
  58.5 15.0 %reduce-scatter.2.cloned.1.call-done = bf16[6,48,301]{2,1,0:T(8,128)(2,1)} async-done(((bf16[6,96,301]{2,1,0:T(8,128)(2,1)}), bf16[6,48,301]{2,1,0:T(8,128)(2,1)}) %reduce-scatter.2.cloned.1.call-update) | async-done | bytes 173392 | tf_op jit(solution)/shard_map/reduce_scatter | solution.py:107
  73.5 1.8 %convert_multiply_fusion = f32[6,48,301]{2,1,0:T(8,128)} fusion(bf16[6,48,301]{2,1,0:T(8,128)(2,1)} %reduce-scatter.2.cloned.1.call-done, f32[6,48]{1,0:T(8,128)S(1)} %convert_element_type.111), kind=kLoop, calls=%fused_computation.37 | loop fusion | flops 173376 | bytes 521280 | tf_op jit(solution)/shard_map/mul | solution.py:110
  (15 shorter events, 0.3 us)
Async XLA Ops:
  6.5 66.9 %reduce-scatter.2.cloned.1.call-start = ((), (), s32[]{:S(2)}) async-start(), calls=%async_computation.1 | async-start | bytes 663552 | tf_op jit(solution)/shard_map/reduce_scatter | solution.py:107
  6.6 25.5 %copy-start = (bf16[6,1,2048]{2,0,1:T(8,128)(2,1)S(1)}, bf16[6,1,2048]{2,0,1:T(8,128)(2,1)}, u32[]{:S(2)}) copy-start(bf16[6,1,2048]{2,0,1:T(8,128)(2,1)} %param.3) | copy-start | bytes 73732
  32.2 1.2 %copy-start.2 = (s32[6]{0:T(128)S(1)}, s32[6]{0:T(128)}, u32[]{:S(2)}) copy-start(s32[6]{0:T(128)} %param.4) | copy-start | bytes 76
  33.5 4.4 %collective-permute-start = (bf16[6,1,1536]{2,0,1:T(8,128)(2,1)S(1)}, bf16[6,1,1536]{2,0,1:T(8,128)(2,1)S(1)}, u32[]{:S(2)}, u32[]{:S(2)}) collective-permute-start(bf16[6,1,1536]{2,0,1:T(8,128)(2,1)S(1)} %get-tuple-element.14), channel_id=1, source_target_pairs={{0,2},{2,0},{4,6},{6,4},{8,10},{10,8},{12,14},{14,12},{16,18},{18,... | collective-permute-start | bytes 55304 | tf_op jit(solution)/shard_map/ppermute | solution.py:15
  37.9 5.0 %collective-permute-start.1 = (bf16[12,1,1536]{2,0,1:T(8,128)(2,1)S(1)}, bf16[12,1,1536]{2,0,1:T(8,128)(2,1)S(1)}, u32[]{:S(2)}, u32[]{:S(2)}) collective-permute-start(bf16[12,1,1536]{2,0,1:T(8,128)(2,1)S(1)} %maximum_select_fusion.6), channel_id=1, source_target_pairs={{0,4},{2,6},{4,0},{6,2},{8,12},{10,14},{12,8},{14,10},{16,20},{18,... | collective-permute-start | bytes 110600 | tf_op jit(solution)/shard_map/ppermute | solution.py:15
  42.9 4.4 %collective-permute-start.2 = (bf16[24,1,1536]{2,0,1:T(8,128)(2,1)S(1)}, bf16[24,1,1536]{2,0,1:T(8,128)(2,1)S(1)}, u32[]{:S(2)}, u32[]{:S(2)}) collective-permute-start(bf16[24,1,1536]{2,0,1:T(8,128)(2,1)S(1)} %maximum_select_fusion.4), channel_id=1, source_target_pairs={{0,8},{2,10},{4,12},{6,14},{8,0},{10,2},{12,4},{14,6},{16,24},{18,... | collective-permute-start | bytes 221192 | tf_op jit(solution)/shard_map/ppermute | solution.py:15
  47.4 8.6 %collective-permute-start.3 = (bf16[48,1,1536]{2,0,1:T(8,128)(2,1)S(1)}, bf16[48,1,1536]{2,0,1:T(8,128)(2,1)S(1)}, u32[]{:S(2)}, u32[]{:S(2)}) collective-permute-start(bf16[48,1,1536]{2,0,1:T(8,128)(2,1)S(1)} %maximum_select_fusion.2), channel_id=1, source_target_pairs={{0,16},{2,18},{4,20},{6,22},{8,24},{10,26},{12,28},{14,30},{16,0},... | collective-permute-start | bytes 442376 | tf_op jit(solution)/shard_map/ppermute | solution.py:15
  56.6 1.9 %copy-start.1 = (s32[6,48]{1,0:T(8,128)S(1)}, s32[6,48]{1,0:T(8,128)}, u32[]{:S(2)}) copy-start(s32[6,48]{1,0:T(8,128)} %param.5) | copy-start | bytes 3460
Sparse Core Ops, SparseCore 0:
  58.6 14.8 reduce-scatter.1
